TPU v7x, 128 devices: a whole 4x4x4 slice. The times are simulated.
128 devices in a mesh: face: 8 (over x, z_hi), tile: 16 (over z_lo, y, core).
Axes of the slice: x: 4, y: 4, z: 4 (z_hi: 2, z_lo: 2; z = z_hi * 2 + z_lo), core: 2. Of those that a mesh axis runs over, the one named last changes fastest.
Arguments:
- state_field: bfloat16 [4, 512, 1024, 256], P(None, 'face', 'tile'), may hold values from -6 to 6
- cotangent: bfloat16 [4, 512, 1024, 256], P(None, 'face', 'tile'), may hold values from -6 to 6
- depth_weight: float32 [9, 256], replicated, may hold values from -2 to 2
- depth_bias: float32 [256], replicated, may hold values from -3 to 3
- point_weight: bfloat16 [256, 256], replicated, may hold values from -0.375 to 0.375
- tile_links: int32 [128, 4], P(('face', 'tile')), may hold values from 0 to 127, as said below
- link_sides: int32 [128, 4], P(('face', 'tile')), may hold values from 0 to 3
- link_flips: int32 [128, 4], P(('face', 'tile')), may hold values from 0 to 1
- corner_masks: int32 [128, 4], P(('face', 'tile')), may hold values 0 or 1
Outputs:
- field_grad: bfloat16 [4, 512, 1024, 256], P(None, 'face', 'tile')
- depth_grad: float32 [9, 256], replicated
- bias_grad: float32 [256], replicated
- point_grad: float32 [256, 256], replicated
Inputs may be any that keep to these rules, and one draw needn't show every extreme that they name: Tile ids number the grid row by row, the row being the index along face. The four neighbours of a tile are the four tiles one step away along face or along tile with wrap-around, each exactly once. Links are mutual: if tile_links[a, s] = b and link_sides[a, s] = o then tile_links[b, o] = a, link_sides[b, o] = s and link_flips[b, o] = link_flips[a, s].
All inputs are finite; a program needn't handle non-finite values. No bound on the sum of `corner_masks` on one device may be relied on, other than what follows from the above.
Results may differ from a plain program's by a relative error of at most 0.0049.
Values may be sent and summed in bfloat16 or wider, within the bound.
No kernel may reach another device: no remote copies, remote signals or barrier semaphores. Data moves between devices by JAX's collectives and lax.ppermute only.
A program may use at most 192 MiB of HBM per device.

v0:
```python
import jax
import jax.numpy as jnp
from jax import lax
from jax.sharding import PartitionSpec as P

root_two_pi = 0.7978845608028654
cubic_coef = 0.044715


def with_halo(block, sides, width):
    for axis, dim in sides:
        count = lax.axis_size(axis)
        forward = [(i, i + 1) for i in range(count - 1)]
        forward.append((count - 1, 0))
        backward = [(target, source) for source, target in forward]
        low = lax.ppermute(
            lax.slice_in_dim(block, block.shape[dim] - width, None, axis=dim), axis, forward
        )
        high = lax.ppermute(lax.slice_in_dim(block, 0, width, axis=dim), axis, backward)
        block = jnp.concatenate([low, block, high], axis=dim)
    return block


def gelu_pair(hidden):
    inside = root_two_pi * (hidden + cubic_coef * hidden * hidden * hidden)
    tanh_val = jnp.tanh(inside)
    output = 0.5 * hidden * (1.0 + tanh_val)
    slope = 0.5 * (1.0 + tanh_val) + 0.5 * hidden * (1.0 - tanh_val * tanh_val) * root_two_pi * (
        1.0 + 3.0 * cubic_coef * hidden * hidden
    )
    return (output, slope)


def edge_rows(block):
    return jnp.stack([block[:, 0], block[:, :, -1], block[:, -1], block[:, :, 0]], axis=0)


def split_dirs(per_dir):
    return (
        jnp.stack([per_dir[0], per_dir[2]], axis=0),
        jnp.stack([per_dir[3], per_dir[1]], axis=0),
    )


def join_dirs(got_face, got_tile):
    return jnp.stack([got_face[0], got_tile[3], got_face[3], got_tile[0]], axis=0)


def padded_tile(block, rim_rows, cmask):
    rim32 = rim_rows.astype(jnp.float32)
    north_west = (cmask[0] * 0.5 * (rim32[0][:, 0] + rim32[3][:, 0])).astype(jnp.bfloat16)
    north_east = (cmask[1] * 0.5 * (rim32[0][:, -1] + rim32[1][:, 0])).astype(jnp.bfloat16)
    south_east = (cmask[2] * 0.5 * (rim32[1][:, -1] + rim32[2][:, -1])).astype(jnp.bfloat16)
    south_west = (cmask[3] * 0.5 * (rim32[2][:, 0] + rim32[3][:, -1])).astype(jnp.bfloat16)
    top_row = jnp.concatenate([north_west[:, None], rim_rows[0], north_east[:, None]], axis=1)
    low_row = jnp.concatenate([south_west[:, None], rim_rows[2], south_east[:, None]], axis=1)
    middle = jnp.concatenate([rim_rows[3][:, :, None], block, rim_rows[1][:, :, None]], axis=2)
    return jnp.concatenate([top_row[:, None], middle, low_row[:, None]], axis=1)


def rim_terms(tap_rows, ext_rows):
    inner_rows = ext_rows[:, :, 1:-1].astype(jnp.float32)
    zero_rows = jnp.zeros_like(inner_rows[:, :, :1])
    padded_rows = jnp.concatenate([zero_rows, inner_rows, zero_rows], axis=2)
    tap_first = tap_rows[:, 0][:, None, None, :]
    tap_middle = tap_rows[:, 1][:, None, None, :]
    tap_last = tap_rows[:, 2][:, None, None, :]
    result = (
        tap_first * padded_rows[:, :, 2:]
        + tap_middle * padded_rows[:, :, 1:-1]
        + tap_last * padded_rows[:, :, :-2]
    )
    result = result.at[:, :, 0].add(
        0.5 * tap_first[:, :, 0] * ext_rows[:, :, 0].astype(jnp.float32)
    )
    result = result.at[:, :, -1].add(
        0.5 * tap_last[:, :, 0] * ext_rows[:, :, -1].astype(jnp.float32)
    )
    return result


def shards(
    state_field,
    cotangent,
    depth_weight,
    depth_bias,
    point_weight,
    tile_links,
    link_sides,
    link_flips,
    corner_masks,
):
    batch_size, tile_side, unused_side, channels = state_field.shape
    face_count = lax.axis_size("face")
    tile_count = lax.axis_size("tile")
    face_pos = lax.axis_index("face")
    tile_pos = lax.axis_index("tile")
    toward = jnp.stack(
        [
            (face_pos - 1) % face_count * tile_count + tile_pos,
            face_pos * tile_count + (tile_pos + 1) % tile_count,
            (face_pos + 1) % face_count * tile_count + tile_pos,
            face_pos * tile_count + (tile_pos - 1) % tile_count,
        ]
    )
    matched = tile_links[0][:, None] == toward[None, :]
    counter = jnp.arange(4, dtype=jnp.int32)
    dir_of_side = jnp.sum(jnp.where(matched, counter[None, :], 0), axis=1)
    side_of_dir = jnp.sum(jnp.where(matched, counter[:, None], 0), axis=0)
    flip_side = (link_flips[0] == 1)[:, None, None, None]
    cmask = corner_masks[0].astype(jnp.float32)
    sending = jnp.take(edge_rows(state_field), side_of_dir, axis=0)
    along_face, along_tile = split_dirs(sending)
    got_face = with_halo(along_face, (("face", 0),), 1)
    got_tile = with_halo(along_tile, (("tile", 0),), 1)
    rim_rows = jnp.take(join_dirs(got_face, got_tile), dir_of_side, axis=0)
    rim_rows = jnp.where(flip_side, rim_rows[:, :, ::-1], rim_rows)
    padded = padded_tile(state_field, rim_rows, cmask)
    tap_table = depth_weight.reshape(3, 3, channels)
    hidden = jnp.zeros(state_field.shape, jnp.float32) + depth_bias
    for row_off in range(3):
        for col_off in range(3):
            hidden = hidden + tap_table[row_off, col_off] * padded[
                :, row_off : row_off + tile_side, col_off : col_off + tile_side
            ].astype(jnp.float32)
    output, slope = gelu_pair(hidden)
    act = output.astype(jnp.bfloat16)
    row_count = batch_size * tile_side * tile_side
    cot_rows = cotangent.reshape(row_count, channels)
    grad_act = lax.dot_general(
        cot_rows, point_weight, (((1,), (1,)), ((), ())), preferred_element_type=jnp.float32
    )
    grad_hidden = (grad_act.reshape(hidden.shape) * slope).astype(jnp.bfloat16)
    point_part = lax.dot_general(
        act.reshape(row_count, channels),
        cot_rows,
        (((0,), (0,)), ((), ())),
        preferred_element_type=jnp.float32,
    )
    grad32 = grad_hidden.astype(jnp.float32)
    depth_list = []
    for row_off in range(3):
        for col_off in range(3):
            window = padded[:, row_off : row_off + tile_side, col_off : col_off + tile_side].astype(
                jnp.float32
            )
            depth_list.append(jnp.sum(grad32 * window, axis=(0, 1, 2)))
    depth_part = jnp.stack(depth_list, axis=0)
    bias_part = jnp.sum(grad32, axis=(0, 1, 2))
    point_sum, depth_sum, bias_sum = lax.psum((point_part, depth_part, bias_part), ("face", "tile"))
    norm_scale = float(batch_size * tile_side * tile_side * face_count * tile_count) ** (-0.5)
    grad_padded = jnp.pad(grad32, ((0, 0), (1, 1), (1, 1), (0, 0)))
    inner_grad = jnp.zeros(state_field.shape, jnp.float32)
    for row_off in range(3):
        for col_off in range(3):
            inner_grad = (
                inner_grad
                + tap_table[row_off, col_off]
                * grad_padded[
                    :, 2 - row_off : 2 - row_off + tile_side, 2 - col_off : 2 - col_off + tile_side
                ]
            )
    side_taps = jnp.stack([tap_table[0], tap_table[:, 2], tap_table[2], tap_table[:, 0]], axis=0)
    low_corner = jnp.array([0, 1, 3, 0], dtype=jnp.int32)
    high_corner = jnp.array([1, 2, 2, 3], dtype=jnp.int32)
    mask_low = jnp.take(corner_masks[0], low_corner).astype(jnp.bfloat16)[:, None, None, None]
    mask_high = jnp.take(corner_masks[0], high_corner).astype(jnp.bfloat16)[:, None, None, None]
    hidden_edges = edge_rows(grad_hidden)
    ext_rows = jnp.concatenate(
        [hidden_edges[:, :, :1] * mask_low, hidden_edges, hidden_edges[:, :, -1:] * mask_high],
        axis=2,
    )
    rim_parts = rim_terms(side_taps, ext_rows)
    outgoing = jnp.take(rim_parts, side_of_dir, axis=0)
    part_face, part_tile = split_dirs(outgoing)
    back_face = with_halo(part_face.astype(jnp.bfloat16), (("face", 0),), 1).astype(part_face.dtype)
    back_tile = with_halo(part_tile.astype(jnp.bfloat16), (("tile", 0),), 1).astype(part_tile.dtype)
    incoming = jnp.take(join_dirs(back_face, back_tile), dir_of_side, axis=0)
    incoming = jnp.where(flip_side, incoming[:, :, ::-1], incoming)
    inner_grad = (
        inner_grad.at[:, 0]
        .add(incoming[0])
        .at[:, :, -1]
        .add(incoming[1])
        .at[:, -1]
        .add(incoming[2])
        .at[:, :, 0]
        .add(incoming[3])
    )
    field_grad = inner_grad.astype(jnp.bfloat16)
    return (field_grad, depth_sum * norm_scale, bias_sum * norm_scale, point_sum * norm_scale)


def solution(mesh):
    in_specs = (
        P(None, "face", "tile", None),
        P(None, "face", "tile", None),
        P(),
        P(),
        P(),
        P(("face", "tile"), None),
        P(("face", "tile"), None),
        P(("face", "tile"), None),
        P(("face", "tile"), None),
    )
    out_specs = (P(None, "face", "tile", None), P(), P(), P())
    return jax.shard_map(shards, mesh=mesh, in_specs=in_specs, out_specs=out_specs, check_vma=False)
```

profile of v0, /device:TPU:1, one launch (start us, length us, event | category | flops | bytes accessed | tf_op | source)
XLA Modules:
  0.0 391.2 jit_solution(6158489630904382677)
XLA Ops:
  8.3 1.0 slice_bitcast_fusion.18
  9.3 11.6 %copy.60 = bf16[4,64,64,256]{3,1,0,2:T(8,128)(2,1)} copy(bf16[4,64,64,256]{3,2,1,0:T(8,128)(2,1)} %param.29) | data formatting | bytes 16777216 | tf_op args[0]
  20.8 1.0 slice_bitcast_fusion.16
  22.7 4.5 %collective-permute-start = (bf16[1,4,64,256]{3,2,1,0:T(8,128)(2,1)S(1)}, bf16[1,4,64,256]{3,2,1,0:T(8,128)(2,1)S(1)}, u32[]{:S(2)}, u32[]{:S(2)}) collective-permute-start(bf16[1,4,64,256]{3,2,1,0:T(8,128)(2,1)S(1)} %get-tuple-element.148), channel_id=1, source_target_pairs={{0,16},{16,32},{32,48},{48,64},{64,80},{80,96},{96,112},{112,0},{1... | collective-permute-start | bytes 393224 | tf_op jit(solution)/shard_map/ppermute | solution.py:16
  27.2 2.1 collective-permute-start.3
  29.3 2.0 collective-permute-start.2
  36.2 1.3 collective-permute-done.2
  39.6 16.4 %maximum_maximum_fusion = (bf16[4,65,66,256]{3,1,0,2:T(8,128)(2,1)S(1)}, bf16[4,65,66,256]{3,1,0,2:T(8,128)(2,1)}) fusion(bf16[4,64,1,256]{3,1,0,2:T(8,128)(2,1)S(1)} %get-tuple-element.145, bf16[4,64,64,256]{3,1,0,2:T(8,128)(2,1)} %copy.60, bf16[4,64,1,256]{3,1,0,2:T(8,128)(2,1)S(1)} %get-tuple-element.146, bf16[4,1,66,256]{3,1,0,2:T(2,128)(2,1)S(1)} %copy.64, ...), kind=kLoop, calls=%fused_computation.78 | loop fusion | flops 70287360 | bytes 26492928 | tf_op jit(solution)/shard_map/concatenate | solution.py:58
  56.0 35.1 %multiply_convert_fusion = (bf16[4,64,64,256]{3,1,0,2:T(8,128)(2,1)}, f32[4,64,64,256]{3,1,0,2:T(8,128)}) fusion(bf16[4,65,66,256]{3,1,0,2:T(8,128)(2,1)} %get-tuple-element.119, f32[256]{0:T(256)S(1)} %bitcast.133, f32[256]{0:T(256)S(1)} %bitcast.135, f32[256]{0:T(256)S(1)} %bitcast.137, bf16[4,64,1,256]{3,1,0,2:T(8,128)(2,1)S(1)} %get-tuple-element.145, ...), kind=kLoop, calls=%fused_computation.77 | loop fusion | flops 159383552 | bytes 84158464 | tf_op jit(solution)/shard_map/convert_element_type | solution.py:127
  91.1 16.0 %fusion.29 = f32[4,64,64,256]{3,1,0,2:T(8,128)} fusion(f32[4,64,64,256]{3,1,0,2:T(8,128)} %get-tuple-element.111), kind=kLoop, calls=%fused_computation.65 | loop fusion | flops 71303168 | bytes 33554432 | tf_op jit(solution)/shard_map/add | solution.py:28
  107.1 25.4 %fusion.39 = bf16[4,64,64,256]{3,2,1,0:T(8,128)(2,1)} fusion(f32[4,64,64,256]{3,1,0,2:T(8,128)} %fusion.29, bf16[4,64,64,256]{3,2,1,0:T(8,128)(2,1)} %param.30, bf16[256,256]{1,0:T(8,128)(2,1)S(1)} %copy-done), kind=kOutput, calls=%fused_computation.76 | convolution fusion | flops 2155872256 | bytes 33685504 | tf_op jit(solution)/shard_map/dot_general | solution.py:130
  132.5 35.5 %fusion.38 = (f32[256]{0:T(256)S(1)}, f32[256]{0:T(256)S(1)}, f32[256]{0:T(256)S(1)}, f32[256]{0:T(256)S(1)}, f32[256]{0:T(256)S(1)}, /*index=5*/f32[256]{0:T(25...) fusion(bf16[4,65,66,256]{3,1,0,2:T(8,128)(2,1)} %get-tuple-element.119, ...), kind=kLoop, calls=%fused_computation.74 | loop fusion | flops 130020864 | bytes 75769856 | tf_op jit(solution)/shard_map/reduce_sum | solution.py:147
  168.1 1.4 slice.591
  169.4 1.0 slice_bitcast_fusion.10
  170.4 12.5 %fusion.78 = (bf16[4,64,64,256]{3,1,0,2:T(8,128)(2,1)}, f32[4,64,64,256]{3,1,0,2:T(8,128)}) fusion(bf16[4,64,64,256]{3,2,1,0:T(8,128)(2,1)} %fusion.39), kind=kLoop, calls=%fused_computation.198 | loop fusion | flops 4194304 | bytes 33554432 | tf_op jit(solution)/shard_map/convert_element_type | solution.py:133
  182.9 15.5 %fusion.43 = f32[256,256]{1,0:T(8,128)} fusion(bf16[4,64,64,256]{3,2,1,0:T(8,128)(2,1)} %param.30, bf16[4,64,64,256]{3,1,0,2:T(8,128)(2,1)} %get-tuple-element.110), kind=kOutput, calls=%fused_computation.87 | convolution fusion | flops 2147483648 | bytes 17039360 | tf_op jit(solution)/shard_map/dot_general | solution.py:134
  198.5 65.7 %all-reduce.3 = (f32[9,256]{1,0:T(8,128)S(1)}, f32[256]{0:T(256)S(1)}) all-reduce(f32[9,256]{1,0:T(8,128)S(1)} %stack.83, f32[256]{0:T(256)S(1)} %get-tuple-element.99), channel_id=1, replica_groups=mesh['face'=8,'tile'=16] {'face','tile'}, use_global_device_ids=true, to_apply=%region_11.15 | all-reduce | flops 2560 | bytes 20480 | tf_op jit(solution)/shard_map/psum | solution.py:150
  264.9 0.9 slice_bitcast_fusion.9
  267.5 1.4 collective-permute-start.4
  268.9 1.0 collective-permute-start.7
  270.6 3.8 collective-permute-start.5
  274.4 51.6 %fusion.8 = f32[4,64,64,256]{3,1,0,2:T(8,128)} fusion(f32[4,64,64,256]{3,1,0,2:T(8,128)} %get-tuple-element.123, f32[256]{0:T(256)S(1)} %bitcast.134, f32[256]{0:T(256)S(1)} %bitcast.136, f32[256]{0:T(256)S(1)} %bitcast.138, f32[256]{0:T(256)S(1)} %bitcast.140, f32[256]{0:T(256)S(1)} %bitcast.142, f32[256]{0:T(256)S(1)} %bitcast.144, f32[256]{0:T(256)S(1)} %bitcast.146, ...), kind=kLoop, calls=%fused_computation.44 | loop fusion | flops 75497472 | bytes 41952256 | tf_op jit(solution)/shard_map/add | solution.py:157
  326.5 12.8 %all-reduce.6.cloned.1.call-done = f32[256,256]{1,0:T(8,128)} async-done(((f32[256,256]{1,0:T(8,128)}), f32[256,256]{1,0:T(8,128)}) %all-reduce.6.cloned.1.call-update) | async-done | bytes 262160 | tf_op jit(solution)/shard_map/psum | solution.py:150
  339.3 1.7 broadcast_multiply_fusion
  342.4 1.9 slice_add_fusion.1
  344.3 6.9 %scatter-add.24 = f32[4,64,64,256]{3,1,0,2:T(8,128)} dynamic-update-slice(f32[4,64,64,256]{3,1,0,2:T(8,128)} %fusion.8, f32[4,1,64,256]{3,1,0,2:T(1,128)S(1)} %slice_add_fusion.1, s32[]{:T(128)} %constant.237.clone.1, s32[]{:T(128)} %constant.237.clone.1, s32[]{:T(128)} %constant.237.clone.1, s32[]{:T(128)} %constant.237.clone.1) | dynamic-update-slice | bytes 524292 | tf_op jit(solution)/shard_map/scatter-add | solution.py:182
  351.2 1.7 fusion.55
  352.9 2.0 slice_add_fusion
  354.9 6.9 %scatter-add.26 = f32[4,64,64,256]{3,1,0,2:T(8,128)} dynamic-update-slice(f32[4,64,64,256]{3,1,0,2:T(8,128)} %fusion.55, f32[4,1,64,256]{3,1,0,2:T(1,128)S(1)} %slice_add_fusion, s32[]{:T(128)} %constant.237.clone.1, s32[]{:T(128)} %constant.249.clone.1, s32[]{:T(128)} %constant.237.clone.1, s32[]{:T(128)} %constant.237.clone.1) | dynamic-update-slice | bytes 524292 | tf_op jit(solution)/shard_map/scatter-add | solution.py:186
  361.8 1.7 fusion.53
  363.5 9.1 %convert_element_type.121 = bf16[4,64,64,256]{3,1,0,2:T(8,128)(2,1)} convert(f32[4,64,64,256]{3,1,0,2:T(8,128)} %fusion.53) | non-fusion elementwise | flops 4194304 | bytes 25165824 | tf_op jit(solution)/shard_map/convert_element_type | solution.py:190
  372.5 11.6 %copy.80 = bf16[4,64,64,256]{3,2,1,0:T(8,128)(2,1)} copy(bf16[4,64,64,256]{3,1,0,2:T(8,128)(2,1)} %convert_element_type.121) | data formatting | bytes 16777216
  (93 shorter events, 11.0 us)
Async XLA Ops:
  7.2 100.0 %copy-start = (bf16[256,256]{1,0:T(8,128)(2,1)S(1)}, bf16[256,256]{1,0:T(8,128)(2,1)}, u32[]{:S(2)}) copy-start(bf16[256,256]{1,0:T(8,128)(2,1)} %param.33) | copy-start | bytes 393220
  7.2 25.0 %copy-start.7 = (s32[4]{0:T(128)S(1)}, s32[4]{0:T(128)}, u32[]{:S(2)}) copy-start(s32[4]{0:T(128)} %constant.280) | copy-start | bytes 52
  7.2 25.0 %copy-start.6 = (s32[4]{0:T(128)S(1)}, s32[4]{0:T(128)}, u32[]{:S(2)}) copy-start(s32[4]{0:T(128)} %constant.281) | copy-start | bytes 52
  7.2 24.3 %copy-start.4 = (f32[9,256]{1,0:T(8,128)S(1)}, f32[9,256]{1,0:T(8,128)}, u32[]{:S(2)}) copy-start(f32[9,256]{1,0:T(8,128)} %param.31) | copy-start | bytes 27652
  7.2 24.3 %copy-start.8 = (s32[1,4]{1,0:T(1,128)S(1)}, s32[1,4]{1,0:T(1,128)}, u32[]{:S(2)}) copy-start(s32[1,4]{1,0:T(1,128)} %param.35) | copy-start | bytes 52
  7.2 24.3 %copy-start.2 = (s32[1,4]{1,0:T(1,128)S(1)}, s32[1,4]{1,0:T(1,128)}, u32[]{:S(2)}) copy-start(s32[1,4]{1,0:T(1,128)} %param.36) | copy-start | bytes 52
  7.2 332.0 %all-reduce.6.cloned.1.call-start = ((), (), s32[]{:S(2)}) async-start(), calls=%async_computation | async-start | bytes 524288 | tf_op jit(solution)/shard_map/psum | solution.py:150
  22.7 13.5 %collective-permute-start = (bf16[1,4,64,256]{3,2,1,0:T(8,128)(2,1)S(1)}, bf16[1,4,64,256]{3,2,1,0:T(8,128)(2,1)S(1)}, u32[]{:S(2)}, u32[]{:S(2)}) collective-permute-start(bf16[1,4,64,256]{3,2,1,0:T(8,128)(2,1)S(1)} %get-tuple-element.148), channel_id=1, source_target_pairs={{0,16},{16,32},{32,48},{48,64},{64,80},{80,96},{96,112},{112,0},{1... | collective-permute-start | bytes 393224 | tf_op jit(solution)/shard_map/ppermute | solution.py:16
  27.2 9.0 %collective-permute-start.3 = (bf16[1,4,64,256]{3,2,1,0:T(8,128)(2,1)S(1)}, bf16[1,4,64,256]{3,2,1,0:T(8,128)(2,1)S(1)}, u32[]{:S(2)}, u32[]{:S(2)}) collective-permute-start(bf16[1,4,64,256]{3,2,1,0:T(8,128)(2,1)S(1)} %get-tuple-element.149), channel_id=1, source_target_pairs={{0,1},{1,2},{2,3},{3,4},{4,5},{5,6},{6,7},{7,8},{8,9},{9,10},{10,1... | collective-permute-start | bytes 393224 | tf_op jit(solution)/shard_map/ppermute | solution.py:16
  29.3 8.2 %collective-permute-start.2 = (bf16[1,4,64,256]{3,2,1,0:T(8,128)(2,1)S(1)}, bf16[1,4,64,256]{3,2,1,0:T(8,128)(2,1)S(1)}, u32[]{:S(2)}, u32[]{:S(2)}) collective-permute-start(bf16[1,4,64,256]{3,2,1,0:T(8,128)(2,1)S(1)} %get-tuple-element.150), channel_id=1, source_target_pairs={{16,0},{32,16},{48,32},{64,48},{80,64},{96,80},{112,96},{0,112},{1... | collective-permute-start | bytes 393224 | tf_op jit(solution)/shard_map/ppermute | solution.py:19
  31.3 6.2 %collective-permute-start.1 = (bf16[1,4,64,256]{3,2,1,0:T(8,128)(2,1)S(1)}, bf16[1,4,64,256]{3,2,1,0:T(8,128)(2,1)S(1)}, u32[]{:S(2)}, u32[]{:S(2)}) collective-permute-start(bf16[1,4,64,256]{3,2,1,0:T(8,128)(2,1)S(1)} %get-tuple-element.151), channel_id=1, source_target_pairs={{1,0},{2,1},{3,2},{4,3},{5,4},{6,5},{7,6},{8,7},{9,8},{10,9},{11,1... | collective-permute-start | bytes 393224 | tf_op jit(solution)/shard_map/ppermute | solution.py:19
  38.9 17.2 %copy-start.5 = (f32[256]{0:T(256)S(1)}, f32[256]{0:T(256)}, u32[]{:S(2)}) copy-start(f32[256]{0:T(256)} %param.32) | copy-start | bytes 3076
  56.0 35.1 %copy-start.3 = (bf16[4,65,66,256]{3,1,0,2:T(8,128)(2,1)}, bf16[4,65,66,256]{3,1,0,2:T(8,128)(2,1)S(1)}, u32[]{:S(2)}) copy-start(bf16[4,65,66,256]{3,1,0,2:T(8,128)(2,1)S(1)} %get-tuple-element.118) | copy-start | bytes 26357764
  267.5 73.5 %collective-permute-start.4 = (bf16[1,4,64,256]{3,2,1,0:T(8,128)(2,1)S(1)}, bf16[1,4,64,256]{3,2,1,0:T(8,128)(2,1)S(1)}, u32[]{:S(2)}, u32[]{:S(2)}) collective-permute-start(bf16[1,4,64,256]{3,2,1,0:T(8,128)(2,1)S(1)} %get-tuple-element.138), channel_id=1, source_target_pairs={{0,16},{16,32},{32,48},{48,64},{64,80},{80,96},{96,112},{112,0},{1... | collective-permute-start | bytes 393224 | tf_op jit(solution)/shard_map/ppermute | solution.py:16
  268.9 72.1 %collective-permute-start.7 = (bf16[1,4,64,256]{3,2,1,0:T(8,128)(2,1)S(1)}, bf16[1,4,64,256]{3,2,1,0:T(8,128)(2,1)S(1)}, u32[]{:S(2)}, u32[]{:S(2)}) collective-permute-start(bf16[1,4,64,256]{3,2,1,0:T(8,128)(2,1)S(1)} %get-tuple-element.139), channel_id=1, source_target_pairs={{1,0},{2,1},{3,2},{4,3},{5,4},{6,5},{7,6},{8,7},{9,8},{10,9},{11,1... | collective-permute-start | bytes 393224 | tf_op jit(solution)/shard_map/ppermute | solution.py:19
  269.9 71.1 %collective-permute-start.6 = (bf16[1,4,64,256]{3,2,1,0:T(8,128)(2,1)S(1)}, bf16[1,4,64,256]{3,2,1,0:T(8,128)(2,1)S(1)}, u32[]{:S(2)}, u32[]{:S(2)}) collective-permute-start(bf16[1,4,64,256]{3,2,1,0:T(8,128)(2,1)S(1)} %get-tuple-element.140), channel_id=1, source_target_pairs={{0,1},{1,2},{2,3},{3,4},{4,5},{5,6},{6,7},{7,8},{8,9},{9,10},{10,1... | collective-permute-start | bytes 393224 | tf_op jit(solution)/shard_map/ppermute | solution.py:16
  270.6 70.4 %collective-permute-start.5 = (bf16[1,4,64,256]{3,2,1,0:T(8,128)(2,1)S(1)}, bf16[1,4,64,256]{3,2,1,0:T(8,128)(2,1)S(1)}, u32[]{:S(2)}, u32[]{:S(2)}) collective-permute-start(bf16[1,4,64,256]{3,2,1,0:T(8,128)(2,1)S(1)} %get-tuple-element.141), channel_id=1, source_target_pairs={{16,0},{32,16},{48,32},{64,48},{80,64},{96,80},{112,96},{0,112},{1... | collective-permute-start | bytes 393224 | tf_op jit(solution)/shard_map/ppermute | solution.py:19
  361.8 22.4 %copy-start.1 = (bf16[256,256]{1,0:T(8,128)(2,1)S(1)}, bf16[256,256]{1,0:T(8,128)(2,1)}, u32[]{:S(2)}) copy-start(bf16[256,256]{1,0:T(8,128)(2,1)} %param.33) | copy-start | bytes 393220
Sparse Core Ops, SparseCore 0:
  198.6 140.6 all-reduce.5
where the time goes:
time: 398 us; the launch traced here: 391 us
  other arithmetic  189 us (47%)
  blocking collectives  65.7 us (17%)
  local copies, waits for them, and re-layouts  48 us (12%)
  matrix products  40.9 us (10%)
  between operations  17.4 us (4%)
  starting transfers between devices  15.7 us (4%)
  waiting for transfers between devices  14.1 us (4%)
    psum x1, blocking collectives, shards(): lax.psum((point_part, depth_part, bias_part), ('face', 'tile'))  65.7 us
    add x1, other arithmetic, shards(): inner_grad + tap_table[row_off, col_off] * grad_padded[:, 2 - row_off:2 -...  51.6 us
    reduce_sum x1, other arithmetic, shards(): depth_list.append(jnp.sum(grad32 * window, axis=(0, 1, 2)))  35.5 us
    convert_element_type x1, other arithmetic, shards(): act = output.astype(jnp.bfloat16)  35.1 us
    dot_general x1, matrix products, shards(): lax.dot_general(cot_rows, point_weight, (((1,), (1,)), ((), ())), preferr...  25.4 us
    unnamed x26, local copies, waits for them, and re-layouts  23.3 us
    concatenate x1, other arithmetic, padded_tile(): return jnp.concatenate([top_row[:, None], middle, low_row[:, None]], axis=1)  16.4 us
    add x1, other arithmetic, gelu_pair(): 0.5 * (1.0 + tanh_val)  16 us
  transfers between devices with their start and end apart: 9, of which 2 were waited for; matrix products, arithmetic and copies ran while one was open for 15% of the time, Pallas kernels for 0%

commit v1 on v0

--- a/solution.py
+++ b/solution.py
@@ -147,7 +147,9 @@
             depth_list.append(jnp.sum(grad32 * window, axis=(0, 1, 2)))
     depth_part = jnp.stack(depth_list, axis=0)
     bias_part = jnp.sum(grad32, axis=(0, 1, 2))
-    point_sum, depth_sum, bias_sum = lax.psum((point_part, depth_part, bias_part), ("face", "tile"))
+    point_sum, depth_sum, bias_sum = lax.psum(
+        lax.psum((point_part, depth_part, bias_part), "tile"), "face"
+    )
     norm_scale = float(batch_size * tile_side * tile_side * face_count * tile_count) ** (-0.5)
     grad_padded = jnp.pad(grad32, ((0, 0), (1, 1), (1, 1), (0, 0)))
     inner_grad = jnp.zeros(state_field.shape, jnp.float32)

time: 398 us -> 464 us (1.17)
  the two profiles are of different devices: /device:TPU:1 before, /device:TPU:0 now
where the time goes in v1:
time: 464 us; the launch traced here: 457 us
  other arithmetic  190 us (41%)
  blocking collectives  95.6 us (21%)
  waiting for transfers between devices  49.2 us (11%)
  local copies, waits for them, and re-layouts  48.2 us (10%)
  matrix products  40.9 us (9%)
  between operations  17.4 us (4%)
  starting transfers between devices  15.7 us (3%)
    psum x1, blocking collectives, shards(): lax.psum((point_part, depth_part, bias_part), 'tile')  55.8 us
    add x1, other arithmetic, shards(): inner_grad + tap_table[row_off, col_off] * grad_padded[:, 2 - row_off:2 -...  51.4 us
    psum x1, waiting for transfers between devices, shards(): lax.psum(lax.psum((point_part, depth_part, bias_part), 'tile'), 'face')  49.1 us
    psum x1, blocking collectives, shards(): lax.psum(lax.psum((point_part, depth_part, bias_part), 'tile'), 'face')  39.8 us
    reduce_sum x1, other arithmetic, shards(): depth_list.append(jnp.sum(grad32 * window, axis=(0, 1, 2)))  36.1 us
    convert_element_type x1, other arithmetic, shards(): act = output.astype(jnp.bfloat16)  35.2 us
    dot_general x1, matrix products, shards(): lax.dot_general(cot_rows, point_weight, (((1,), (1,)), ((), ())), preferr...  25.4 us
    unnamed x26, local copies, waits for them, and re-layouts  23.3 us
  transfers between devices with their start and end apart: 10, of which 1 were waited for; matrix products, arithmetic and copies ran while one was open for 22% of the time, Pallas kernels for 0%

profile of v1, /device:TPU:0, one launch (start us, length us, event | category | flops | bytes accessed | tf_op | source)
XLA Modules:
  0.0 457.1 jit_solution(6691218395453377960)
XLA Ops:
  7.4 0.8 fusion.74
  8.3 1.0 slice_bitcast_fusion.18
  9.3 11.6 %copy.60 = bf16[4,64,64,256]{3,1,0,2:T(8,128)(2,1)} copy(bf16[4,64,64,256]{3,2,1,0:T(8,128)(2,1)} %param.29) | data formatting | bytes 16777216 | tf_op args[0]
  20.8 1.0 slice_bitcast_fusion.16
  22.7 4.0 collective-permute-start
  26.7 2.4 collective-permute-start.2
  29.0 3.0 collective-permute-start.1
  32.2 0.7 fusion.83
  39.0 16.4 %maximum_maximum_fusion = (bf16[4,65,66,256]{3,1,0,2:T(8,128)(2,1)S(1)}, bf16[4,65,66,256]{3,1,0,2:T(8,128)(2,1)}) fusion(bf16[4,64,1,256]{3,1,0,2:T(8,128)(2,1)S(1)} %get-tuple-element.147, bf16[4,64,64,256]{3,1,0,2:T(8,128)(2,1)} %copy.60, bf16[4,64,1,256]{3,1,0,2:T(8,128)(2,1)S(1)} %get-tuple-element.148, bf16[4,1,66,256]{3,1,0,2:T(2,128)(2,1)S(1)} %copy.64, ...), kind=kLoop, calls=%fused_computation.78 | loop fusion | flops 70287360 | bytes 26492928 | tf_op jit(solution)/shard_map/concatenate | solution.py:58
  55.4 35.2 %multiply_convert_fusion = (bf16[4,64,64,256]{3,1,0,2:T(8,128)(2,1)}, f32[4,64,64,256]{3,1,0,2:T(8,128)}) fusion(bf16[4,65,66,256]{3,1,0,2:T(8,128)(2,1)} %get-tuple-element.121, f32[256]{0:T(256)S(1)} %bitcast.133, f32[256]{0:T(256)S(1)} %bitcast.135, f32[256]{0:T(256)S(1)} %bitcast.137, bf16[4,64,1,256]{3,1,0,2:T(8,128)(2,1)S(1)} %get-tuple-element.147, ...), kind=kLoop, calls=%fused_computation.77 | loop fusion | flops 159383552 | bytes 84158464 | tf_op jit(solution)/shard_map/convert_element_type | solution.py:127
  90.6 16.0 %fusion.29 = f32[4,64,64,256]{3,1,0,2:T(8,128)} fusion(f32[4,64,64,256]{3,1,0,2:T(8,128)} %get-tuple-element.113), kind=kLoop, calls=%fused_computation.65 | loop fusion | flops 71303168 | bytes 33554432 | tf_op jit(solution)/shard_map/add | solution.py:28
  106.6 25.4 %fusion.39 = bf16[4,64,64,256]{3,2,1,0:T(8,128)(2,1)} fusion(f32[4,64,64,256]{3,1,0,2:T(8,128)} %fusion.29, bf16[4,64,64,256]{3,2,1,0:T(8,128)(2,1)} %param.30, bf16[256,256]{1,0:T(8,128)(2,1)S(1)} %copy-done), kind=kOutput, calls=%fused_computation.76 | convolution fusion | flops 2155872256 | bytes 33685504 | tf_op jit(solution)/shard_map/dot_general | solution.py:130
  132.0 36.1 %fusion.38 = (f32[256]{0:T(256)S(1)}, f32[256]{0:T(256)S(1)}, f32[256]{0:T(256)S(1)}, f32[256]{0:T(256)S(1)}, f32[256]{0:T(256)S(1)}, /*index=5*/f32[256]{0:T(25...) fusion(bf16[4,65,66,256]{3,1,0,2:T(8,128)(2,1)} %get-tuple-element.121, ...), kind=kLoop, calls=%fused_computation.74 | loop fusion | flops 130020864 | bytes 75769856 | tf_op jit(solution)/shard_map/reduce_sum | solution.py:147
  168.1 1.4 slice.591
  169.5 1.0 slice_bitcast_fusion.10
  170.5 12.5 %fusion.78 = (bf16[4,64,64,256]{3,1,0,2:T(8,128)(2,1)}, f32[4,64,64,256]{3,1,0,2:T(8,128)}) fusion(bf16[4,64,64,256]{3,2,1,0:T(8,128)(2,1)} %fusion.39), kind=kLoop, calls=%fused_computation.198 | loop fusion | flops 4194304 | bytes 33554432 | tf_op jit(solution)/shard_map/convert_element_type | solution.py:133
  183.0 15.5 %fusion.43 = f32[256,256]{1,0:T(8,128)} fusion(bf16[4,64,64,256]{3,2,1,0:T(8,128)(2,1)} %param.30, bf16[4,64,64,256]{3,1,0,2:T(8,128)(2,1)} %get-tuple-element.112), kind=kOutput, calls=%fused_computation.87 | convolution fusion | flops 2147483648 | bytes 17039360 | tf_op jit(solution)/shard_map/dot_general | solution.py:134
  198.6 55.8 %all-reduce.3 = (f32[9,256]{1,0:T(8,128)S(1)}, f32[256]{0:T(256)S(1)}) all-reduce(f32[9,256]{1,0:T(8,128)S(1)} %stack.83, f32[256]{0:T(256)S(1)} %get-tuple-element.99), channel_id=1, replica_groups=mesh['face'=8,'tile'=16] {'tile'}, use_global_device_ids=true, to_apply=%region_11.15 | all-reduce | flops 2560 | bytes 20480 | tf_op jit(solution)/shard_map/psum | solution.py:151
  254.4 39.8 %all-reduce.4 = (f32[9,256]{1,0:T(8,128)S(1)}, f32[256]{0:T(256)S(1)}) all-reduce(f32[9,256]{1,0:T(8,128)S(1)} %get-tuple-element.108, f32[256]{0:T(256)S(1)} %get-tuple-element.109), channel_id=1, replica_groups=mesh['face'=8,'tile'=16] {'face'}, use_global_device_ids=true, to_apply=%region_12.16 | all-reduce | flops 2560 | bytes 20480 | tf_op jit(solution)/shard_map/psum | solution.py:150
  294.9 0.9 slice_bitcast_fusion.9
  298.4 5.6 %collective-permute-start.5 = (bf16[1,4,64,256]{3,2,1,0:T(8,128)(2,1)S(1)}, bf16[1,4,64,256]{3,2,1,0:T(8,128)(2,1)S(1)}, u32[]{:S(2)}, u32[]{:S(2)}) collective-permute-start(bf16[1,4,64,256]{3,2,1,0:T(8,128)(2,1)S(1)} %get-tuple-element.143), channel_id=1, source_target_pairs={{16,0},{32,16},{48,32},{64,48},{80,64},{96,80},{112,96},{0,112},{1... | collective-permute-start | bytes 393224 | tf_op jit(solution)/shard_map/ppermute | solution.py:19
  303.9 51.4 %fusion.8 = f32[4,64,64,256]{3,1,0,2:T(8,128)} fusion(f32[4,64,64,256]{3,1,0,2:T(8,128)} %get-tuple-element.125, f32[256]{0:T(256)S(1)} %bitcast.134, f32[256]{0:T(256)S(1)} %bitcast.136, f32[256]{0:T(256)S(1)} %bitcast.138, f32[256]{0:T(256)S(1)} %bitcast.140, f32[256]{0:T(256)S(1)} %bitcast.142, f32[256]{0:T(256)S(1)} %bitcast.144, f32[256]{0:T(256)S(1)} %bitcast.146, ...), kind=kLoop, calls=%fused_computation.44 | loop fusion | flops 75497472 | bytes 41952256 | tf_op jit(solution)/shard_map/add | solution.py:159
  357.4 1.9 slice_add_fusion.1
  359.3 6.8 %scatter-add.24 = f32[4,64,64,256]{3,1,0,2:T(8,128)} dynamic-update-slice(f32[4,64,64,256]{3,1,0,2:T(8,128)} %fusion.8, f32[4,1,64,256]{3,1,0,2:T(1,128)S(1)} %slice_add_fusion.1, s32[]{:T(128)} %constant.237.clone.1, s32[]{:T(128)} %constant.237.clone.1, s32[]{:T(128)} %constant.237.clone.1, s32[]{:T(128)} %constant.237.clone.1) | dynamic-update-slice | bytes 524292 | tf_op jit(solution)/shard_map/scatter-add | solution.py:184
  366.1 1.7 fusion.55
  367.8 2.0 slice_add_fusion
  369.8 6.9 %scatter-add.26 = f32[4,64,64,256]{3,1,0,2:T(8,128)} dynamic-update-slice(f32[4,64,64,256]{3,1,0,2:T(8,128)} %fusion.55, f32[4,1,64,256]{3,1,0,2:T(1,128)S(1)} %slice_add_fusion, s32[]{:T(128)} %constant.237.clone.1, s32[]{:T(128)} %constant.249.clone.1, s32[]{:T(128)} %constant.237.clone.1, s32[]{:T(128)} %constant.237.clone.1) | dynamic-update-slice | bytes 524292 | tf_op jit(solution)/shard_map/scatter-add | solution.py:188
  376.7 1.7 fusion.53
  378.4 9.1 %convert_element_type.121 = bf16[4,64,64,256]{3,1,0,2:T(8,128)(2,1)} convert(f32[4,64,64,256]{3,1,0,2:T(8,128)} %fusion.53) | non-fusion elementwise | flops 4194304 | bytes 25165824 | tf_op jit(solution)/shard_map/convert_element_type | solution.py:192
  387.5 11.7 %copy.80 = bf16[4,64,64,256]{3,2,1,0:T(8,128)(2,1)} copy(bf16[4,64,64,256]{3,1,0,2:T(8,128)(2,1)} %convert_element_type.121) | data formatting | bytes 16777216
  399.2 49.1 %all-reduce.10.cloned.1.call-done = f32[256,256]{1,0:T(8,128)} async-done(((f32[256,256]{1,0:T(8,128)}), f32[256,256]{1,0:T(8,128)}) %all-reduce.10.cloned.1.call-update) | async-done | bytes 262160 | tf_op jit(solution)/shard_map/psum | solution.py:150
  448.4 1.7 broadcast_multiply_fusion
  (97 shorter events, 9.6 us)
Async XLA Ops:
  7.2 99.4 %copy-start = (bf16[256,256]{1,0:T(8,128)(2,1)S(1)}, bf16[256,256]{1,0:T(8,128)(2,1)}, u32[]{:S(2)}) copy-start(bf16[256,256]{1,0:T(8,128)(2,1)} %param.33) | copy-start | bytes 393220
  7.2 25.7 %copy-start.7 = (s32[4]{0:T(128)S(1)}, s32[4]{0:T(128)}, u32[]{:S(2)}) copy-start(s32[4]{0:T(128)} %constant.280) | copy-start | bytes 52
  7.2 25.7 %copy-start.6 = (s32[4]{0:T(128)S(1)}, s32[4]{0:T(128)}, u32[]{:S(2)}) copy-start(s32[4]{0:T(128)} %constant.281) | copy-start | bytes 52
  7.2 24.9 %copy-start.4 = (f32[9,256]{1,0:T(8,128)S(1)}, f32[9,256]{1,0:T(8,128)}, u32[]{:S(2)}) copy-start(f32[9,256]{1,0:T(8,128)} %param.31) | copy-start | bytes 27652
  7.2 25.0 %copy-start.8 = (s32[1,4]{1,0:T(1,128)S(1)}, s32[1,4]{1,0:T(1,128)}, u32[]{:S(2)}) copy-start(s32[1,4]{1,0:T(1,128)} %param.35) | copy-start | bytes 52
  7.2 25.0 %copy-start.2 = (s32[1,4]{1,0:T(1,128)S(1)}, s32[1,4]{1,0:T(1,128)}, u32[]{:S(2)}) copy-start(s32[1,4]{1,0:T(1,128)} %param.36) | copy-start | bytes 52
  7.2 360.5 %all-reduce.8.cloned.1.call-start = ((), (), s32[]{:S(2)}) async-start(), calls=%async_computation | async-start | bytes 524288 | tf_op jit(solution)/shard_map/psum | solution.py:151
  22.7 14.2 %collective-permute-start = (bf16[1,4,64,256]{3,2,1,0:T(8,128)(2,1)S(1)}, bf16[1,4,64,256]{3,2,1,0:T(8,128)(2,1)S(1)}, u32[]{:S(2)}, u32[]{:S(2)}) collective-permute-start(bf16[1,4,64,256]{3,2,1,0:T(8,128)(2,1)S(1)} %get-tuple-element.150), channel_id=1, source_target_pairs={{0,16},{16,32},{32,48},{48,64},{64,80},{80,96},{96,112},{112,0},{1... | collective-permute-start | bytes 393224 | tf_op jit(solution)/shard_map/ppermute | solution.py:16
  26.7 10.2 %collective-permute-start.3 = (bf16[1,4,64,256]{3,2,1,0:T(8,128)(2,1)S(1)}, bf16[1,4,64,256]{3,2,1,0:T(8,128)(2,1)S(1)}, u32[]{:S(2)}, u32[]{:S(2)}) collective-permute-start(bf16[1,4,64,256]{3,2,1,0:T(8,128)(2,1)S(1)} %get-tuple-element.151), channel_id=1, source_target_pairs={{0,1},{1,2},{2,3},{3,4},{4,5},{5,6},{6,7},{7,8},{8,9},{9,10},{10,1... | collective-permute-start | bytes 393224 | tf_op jit(solution)/shard_map/ppermute | solution.py:16
  26.7 10.2 %collective-permute-start.2 = (bf16[1,4,64,256]{3,2,1,0:T(8,128)(2,1)S(1)}, bf16[1,4,64,256]{3,2,1,0:T(8,128)(2,1)S(1)}, u32[]{:S(2)}, u32[]{:S(2)}) collective-permute-start(bf16[1,4,64,256]{3,2,1,0:T(8,128)(2,1)S(1)} %get-tuple-element.152), channel_id=1, source_target_pairs={{16,0},{32,16},{48,32},{64,48},{80,64},{96,80},{112,96},{0,112},{1... | collective-permute-start | bytes 393224 | tf_op jit(solution)/shard_map/ppermute | solution.py:19
  29.0 7.8 %collective-permute-start.1 = (bf16[1,4,64,256]{3,2,1,0:T(8,128)(2,1)S(1)}, bf16[1,4,64,256]{3,2,1,0:T(8,128)(2,1)S(1)}, u32[]{:S(2)}, u32[]{:S(2)}) collective-permute-start(bf16[1,4,64,256]{3,2,1,0:T(8,128)(2,1)S(1)} %get-tuple-element.153), channel_id=1, source_target_pairs={{1,0},{2,1},{3,2},{4,3},{5,4},{6,5},{7,6},{8,7},{9,8},{10,9},{11,1... | collective-permute-start | bytes 393224 | tf_op jit(solution)/shard_map/ppermute | solution.py:19
  38.2 17.1 %copy-start.5 = (f32[256]{0:T(256)S(1)}, f32[256]{0:T(256)}, u32[]{:S(2)}) copy-start(f32[256]{0:T(256)} %param.32) | copy-start | bytes 3076
  55.4 35.2 %copy-start.3 = (bf16[4,65,66,256]{3,1,0,2:T(8,128)(2,1)}, bf16[4,65,66,256]{3,1,0,2:T(8,128)(2,1)S(1)}, u32[]{:S(2)}) copy-start(bf16[4,65,66,256]{3,1,0,2:T(8,128)(2,1)S(1)} %get-tuple-element.120) | copy-start | bytes 26357764
  198.5 249.8 %all-reduce.10.cloned.1.call-start = ((), (), s32[]{:S(2)}) async-start(), calls=%async_computation.1 | async-start | bytes 524288 | tf_op jit(solution)/shard_map/psum | solution.py:150
  297.7 58.2 %collective-permute-start.4 = (bf16[1,4,64,256]{3,2,1,0:T(8,128)(2,1)S(1)}, bf16[1,4,64,256]{3,2,1,0:T(8,128)(2,1)S(1)}, u32[]{:S(2)}, u32[]{:S(2)}) collective-permute-start(bf16[1,4,64,256]{3,2,1,0:T(8,128)(2,1)S(1)} %get-tuple-element.140), channel_id=1, source_target_pairs={{0,16},{16,32},{32,48},{48,64},{64,80},{80,96},{96,112},{112,0},{1... | collective-permute-start | bytes 393224 | tf_op jit(solution)/shard_map/ppermute | solution.py:16
  297.8 58.1 %collective-permute-start.7 = (bf16[1,4,64,256]{3,2,1,0:T(8,128)(2,1)S(1)}, bf16[1,4,64,256]{3,2,1,0:T(8,128)(2,1)S(1)}, u32[]{:S(2)}, u32[]{:S(2)}) collective-permute-start(bf16[1,4,64,256]{3,2,1,0:T(8,128)(2,1)S(1)} %get-tuple-element.141), channel_id=1, source_target_pairs={{1,0},{2,1},{3,2},{4,3},{5,4},{6,5},{7,6},{8,7},{9,8},{10,9},{11,1... | collective-permute-start | bytes 393224 | tf_op jit(solution)/shard_map/ppermute | solution.py:19
  297.9 58.0 %collective-permute-start.6 = (bf16[1,4,64,256]{3,2,1,0:T(8,128)(2,1)S(1)}, bf16[1,4,64,256]{3,2,1,0:T(8,128)(2,1)S(1)}, u32[]{:S(2)}, u32[]{:S(2)}) collective-permute-start(bf16[1,4,64,256]{3,2,1,0:T(8,128)(2,1)S(1)} %get-tuple-element.142), channel_id=1, source_target_pairs={{0,1},{1,2},{2,3},{3,4},{4,5},{5,6},{6,7},{7,8},{8,9},{9,10},{10,1... | collective-permute-start | bytes 393224 | tf_op jit(solution)/shard_map/ppermute | solution.py:16
  298.4 57.6 %collective-permute-start.5 = (bf16[1,4,64,256]{3,2,1,0:T(8,128)(2,1)S(1)}, bf16[1,4,64,256]{3,2,1,0:T(8,128)(2,1)S(1)}, u32[]{:S(2)}, u32[]{:S(2)}) collective-permute-start(bf16[1,4,64,256]{3,2,1,0:T(8,128)(2,1)S(1)} %get-tuple-element.143), channel_id=1, source_target_pairs={{16,0},{32,16},{48,32},{64,48},{80,64},{96,80},{112,96},{0,112},{1... | collective-permute-start | bytes 393224 | tf_op jit(solution)/shard_map/ppermute | solution.py:19
  376.7 73.4 %copy-start.1 = (bf16[256,256]{1,0:T(8,128)(2,1)S(1)}, bf16[256,256]{1,0:T(8,128)(2,1)}, u32[]{:S(2)}) copy-start(bf16[256,256]{1,0:T(8,128)(2,1)} %param.33) | copy-start | bytes 393220
Sparse Core Ops, SparseCore 0:
  198.7 115.8 all-reduce.7
  367.9 80.3 all-reduce.9
